TPU v7x, 512 devices: a whole 4x4x16 slice. The times are simulated.
512 devices in a mesh: call: 64 (over z, y_hi, core), tensor: 8 (over x, y_lo).
Axes of the slice: x: 4, y: 4 (y_hi: 2, y_lo: 2; y = y_hi * 2 + y_lo), z: 16, core: 2. Of those that a mesh axis runs over, the one named last changes fastest.
Arguments:
- queries: bfloat16 [64, 768, 8192], P('call', None, 'tensor'), may hold values from -8 to 8
- child_kv: bfloat16 [64, 2, 768, 1024], P('call', None, None, 'tensor'), may hold values from -6 to 6
- summ_kv: bfloat16 [64, 2, 256, 1024], P('call', None, None, 'tensor'), may hold values from -6 to 6
- instr_pool: bfloat16 [64, 1024, 2, 1024], P('call', 'tensor'), may hold values from -16 to 16
- child_len: int32 [64], P('call'), may hold values from 256 to 768, as said below
- summ_len: int32 [64], P('call'), may hold values from 64 to 256, as said below
- owner_group: int32 [1], replicated, may hold values from 0 to 63
Outputs:
- attended: bfloat16 [64, 768, 8192], P('call', None, 'tensor')
Inputs may be any that keep to these rules, and one draw needn't show every extreme that they name: `child_len`: one call has exactly 768 child tokens and one exactly 256. `summ_len`: one call has exactly 256 summary tokens and one exactly 64.
All inputs are finite; a program needn't handle non-finite values.
Results may differ from a plain program's by a relative error of at most 0.006.
Values may be sent and summed in bfloat16 or wider, within the bound.
A program may use at most 64 MiB of HBM per device.

v0:
```python
import math
import jax
import jax.numpy as jnp
from jax import lax
from jax.sharding import PartitionSpec as P

HD = 128
NEG = -1e30


def broadcast(value, axis, source):
    kept = jnp.where(lax.axis_index(axis) == source, value, 0).astype(value.dtype)
    return lax.psum(kept, axis)


def passed_along(block, axis, distance):
    devices = range(lax.axis_size(axis))
    route = [(i - distance, i) for i in devices if i - distance in devices]
    return lax.ppermute(block, axis, route)


def head_split(packed, heads):
    total = packed.shape[0]
    width = packed.shape[1]
    return packed.reshape(total, heads, width // heads).transpose(1, 0, 2)


def partial_softmax(query_head, key_rows, value_rows, allowed):
    score_scale = 1.0 / math.sqrt(query_head.shape[1])
    scores = (
        lax.dot_general(
            query_head, key_rows, (((1,), (1,)), ((), ())), preferred_element_type=jnp.float32
        )
        * score_scale
    )
    scores = jnp.where(allowed, scores, NEG)
    maxima = jnp.max(scores, axis=1, keepdims=True)
    expons = jnp.where(allowed, jnp.exp(scores - maxima), 0.0)
    totals = jnp.sum(expons, axis=1, keepdims=True)
    weights = expons.astype(jnp.bfloat16)
    return (maxima, totals, jnp.dot(weights, value_rows, preferred_element_type=jnp.float32))


def over_heads(query_heads, key_heads, value_heads, allowed):
    group = query_heads.shape[0] // key_heads.shape[0]

    def single(pair):
        query_head, number = pair
        key_rows = lax.dynamic_index_in_dim(key_heads, number // group, 0, keepdims=False)
        value_rows = lax.dynamic_index_in_dim(value_heads, number // group, 0, keepdims=False)
        return partial_softmax(query_head, key_rows, value_rows, allowed)

    return lax.map(single, (query_heads, jnp.arange(query_heads.shape[0], dtype=jnp.int32)))


def shards(queries, child_kv, summ_kv, instr_pool, child_len, summ_len, owner_group):
    query_mat = queries[0]
    length = query_mat.shape[0]
    heads = query_mat.shape[1] // HD
    kv_heads = child_kv.shape[3] // HD
    fetched = broadcast(instr_pool, "call", owner_group[0])
    instr_local = lax.all_to_all(fetched, "tensor", split_axis=3, concat_axis=1, tiled=True)
    sibling_kv, sibling_len = passed_along((summ_kv, summ_len), "call", 1)
    instr_count = instr_local.shape[1]
    summ_count = summ_kv.shape[2]
    positions = jnp.arange(length, dtype=jnp.int32)
    own_allowed = positions[None, :] <= positions[:, None]
    remote_allowed = jnp.concatenate(
        [
            jnp.ones((length, instr_count), bool),
            jnp.broadcast_to(
                jnp.arange(summ_count, dtype=jnp.int32)[None, :] < sibling_len[0],
                (length, summ_count),
            ),
        ],
        1,
    )
    remote_keys = jnp.concatenate([instr_local[0, :, 0], sibling_kv[0, 0]], 0)
    remote_values = jnp.concatenate([instr_local[0, :, 1], sibling_kv[0, 1]], 0)
    query_heads = head_split(query_mat, heads)
    key_all = jnp.concatenate([remote_keys, child_kv[0, 0]], 0)
    value_all = jnp.concatenate([remote_values, child_kv[0, 1]], 0)
    allowed = jnp.concatenate([remote_allowed, own_allowed], 1)
    maxima, totals, sums = over_heads(
        query_heads, head_split(key_all, kv_heads), head_split(value_all, kv_heads), allowed
    )
    combined = sums / totals
    result = combined.transpose(1, 0, 2).reshape(length, heads * HD)
    result = jnp.where((positions < child_len[0])[:, None], result, 0.0)
    return result.astype(jnp.bfloat16)[None]


def solution(mesh):
    in_specs = (
        P("call", None, "tensor"),
        P("call", None, None, "tensor"),
        P("call", None, None, "tensor"),
        P("call", "tensor", None, None),
        P("call"),
        P("call"),
        P(),
    )
    out_specs = P("call", None, "tensor")
    return jax.shard_map(shards, mesh=mesh, in_specs=in_specs, out_specs=out_specs, check_vma=False)
```

profile of v0, /device:TPU:8, one launch (start us, length us, event | category | flops | bytes accessed | tf_op | source)
XLA Modules:
  0.0 634.9 jit_solution(1127240871721148693)
XLA Ops:
  6.5 0.0 all-reduce.2.cloned.1.call-start
  6.5 0.0 copy-start
  6.5 2.8 copy.22
  10.0 1.2 broadcast_select_fusion
  11.2 0.0 all-reduce.2.cloned.1.call-update
  11.2 1.7 collective-permute-start
  13.0 5.0 collective-permute-start.1
  18.0 0.2 iota_compare_fusion
  18.2 2.6 copy.21
  21.4 0.0 copy-done
  21.5 0.0 collective-permute-done.1
  21.5 0.6 iota_compare_fusion.2
  22.1 525.9 %all-reduce.2.cloned.1.call-done = bf16[1,128,2,1024]{1,2,0,3:T(2,128)(2,1)} async-done(((bf16[1,128,2,1024]{1,2,0,3:T(2,128)(2,1)}), bf16[1,128,2,1024]{1,2,0,3:T(2,128)(2,1)}) %all-reduce.2.cloned.1.call-update) | async-done | bytes 524304 | tf_op jit(solution)/shard_map/psum | solution.py:13
  548.0 5.7 all-to-all-start
  553.7 0.6 pad_add_fusion
  554.3 0.0 collective-permute-done
  554.3 8.1 %all-to-all-done = bf16[1,128,2,1024]{1,2,0,3:T(2,128)(2,1)S(1)} async-done(((bf16[1,128,2,1024]{1,2,0,3:T(2,128)(2,1)}), bf16[1,128,2,1024]{1,2,0,3:T(2,128)(2,1)S(1)}, u32[]{:S(2)}, u32[]{:S(2)}) %all-to-all-start) | async-done | bytes 524320 | tf_op jit(solution)/shard_map/all_to_all | solution.py:62
  562.4 0.5 copy.23
  562.9 0.1 maximum_bitcast_fusion
  563.0 59.4 %while.13 = (s32[]{:T(128)}, f32[8,768,1]{1,0,2:T(8,128)S(1)}, f32[8,768,128]{2,1,0:T(8,128)}, bf16[8,768,128]{1,2,0:T(8,128)(2,1)}, bf16[1,2048,128]{2,1,0:T(8,...) while((s32[]{:T(128)}, f32[8,768,1]{1,0,2:T(8,128)S(1)}, ...), condition=%wide.region_4.5_spmd, body=%wide.region_1.4_spmd.sunk | while | flops 825752064 | bytes 25257056 | solution.py:53
  563.0 2.5 fusion.27
  565.5 2.5 fusion.29
  568.0 2.3 fusion.28
  570.3 0.1 dynamic_update_slice.14
  570.4 2.5 fusion.27
  572.9 2.5 fusion.29
  575.4 2.3 fusion.28
  577.7 0.1 dynamic_update_slice.14
  577.8 2.5 fusion.27
  580.3 2.5 fusion.29
  582.8 2.3 fusion.28
  585.1 0.1 dynamic_update_slice.14
  585.3 2.5 fusion.27
  587.7 2.5 fusion.29
  590.3 2.3 fusion.28
  592.6 0.1 dynamic_update_slice.14
  592.7 2.5 fusion.27
  595.2 2.5 fusion.29
  597.7 2.3 fusion.28
  600.0 0.1 dynamic_update_slice.14
  600.1 2.5 fusion.27
  602.6 2.5 fusion.29
  605.1 2.3 fusion.28
  607.5 0.1 dynamic_update_slice.14
  607.6 2.5 fusion.27
  610.1 2.5 fusion.29
  612.6 2.3 fusion.28
  614.9 0.1 dynamic_update_slice.14
  615.0 2.5 fusion.27
  617.5 2.5 fusion.29
  620.0 2.3 fusion.28
  622.3 0.1 dynamic_update_slice.14
  622.4 2.4 divide_bitcast_fusion
  624.8 1.0 copy.25
  625.9 0.7 reshape.46
  626.6 1.5 select_convert_fusion
  (16 shorter events, 0.1 us)
Async XLA Ops:
  6.5 541.5 %all-reduce.2.cloned.1.call-start = ((), (), s32[]{:S(2)}) async-start(), calls=%async_computation.1 | async-start | bytes 1048576 | tf_op jit(solution)/shard_map/psum | solution.py:13
  6.5 14.9 %copy-start = (bf16[1,2,768,128]{3,2,1,0:T(8,128)(2,1)S(1)}, bf16[1,2,768,128]{3,2,1,0:T(8,128)(2,1)}, u32[]{:S(2)}) copy-start(bf16[1,2,768,128]{3,2,1,0:T(8,128)(2,1)} %param.10) | copy-start | bytes 1179652
  11.2 543.0 %collective-permute-start = (bf16[1,2,256,128]{3,2,1,0:T(8,128)(2,1)}, bf16[1,2,256,128]{3,2,1,0:T(8,128)(2,1)S(1)}, u32[]{:S(2)}, u32[]{:S(2)}) collective-permute-start(bf16[1,2,256,128]{3,2,1,0:T(8,128)(2,1)} %param.11), channel_id=1, source_target_pairs={{0,8},{8,16},{16,24},{24,32},{32,40},{40,48},{48,56},{56,64},{64,7... | collective-permute-start | bytes 393224 | tf_op jit(solution)/shard_map/ppermute | solution.py:19
  13.0 8.5 %collective-permute-start.1 = (s32[1]{0:T(128)}, s32[1]{0:T(128)}, u32[]{:S(2)}, u32[]{:S(2)}) collective-permute-start(s32[1]{0:T(128)} %param.14), channel_id=1, source_target_pairs={{0,8},{8,16},{16,24},{24,32},{32,40},{40,48},{48,56},{56,64},{64,7... | collective-permute-start | bytes 20 | tf_op jit(solution)/shard_map/ppermute | solution.py:19
  548.0 14.4 %all-to-all-start = ((bf16[1,128,2,1024]{1,2,0,3:T(2,128)(2,1)}), bf16[1,128,2,1024]{1,2,0,3:T(2,128)(2,1)S(1)}, u32[]{:S(2)}, u32[]{:S(2)}) async-start(bf16[1,128,2,1024]{1,2,0,3:T(2,128)(2,1)} %all-reduce.2.cloned.1.call-done), calls=%async_computation | async-start | bytes 1048576 | tf_op jit(solution)/shard_map/all_to_all | solution.py:62
Sparse Core Ops, SparseCore 0:
  11.4 536.5 all-reduce.1
where the time goes:
time: 635 us
  waiting for transfers between devices  534 us (84%)
  matrix products  40.1 us (6%)
  other arithmetic  24.9 us (4%)
  between operations  14.8 us (2%)
  starting transfers between devices  12.5 us (2%)
  local copies, waits for them, and re-layouts  8.4 us (1%)
    psum x1, waiting for transfers between devices, broadcast(): return lax.psum(kept, axis)  526 us
    dot_general x8, matrix products, partial_softmax(): jnp.dot(weights, value_rows, preferred_element_type=jnp.float32)  20.2 us
    dot_general x8, matrix products, partial_softmax(): lax.dot_general(query_head, key_rows, (((1,), (1,)), ((), ())), preferred...  19.9 us
    reduce_sum x8, other arithmetic, partial_softmax(): totals = jnp.sum(expons, axis=1, keepdims=True)  18.4 us
  transfers between devices with their start and end apart: 4, of which 2 were waited for; matrix products, arithmetic and copies ran while one was open for 1% of the time, Pallas kernels for 0%

commit v1 on v0

--- a/solution.py
+++ b/solution.py
@@ -8,9 +8,13 @@
 NEG = -1e30
 
 
+def begin_the_plane(ax_name, local_block):
+    return jax.lax.all_gather(local_block, ax_name).sum(axis=0)
+
+
 def broadcast(value, axis, source):
     kept = jnp.where(lax.axis_index(axis) == source, value, 0).astype(value.dtype)
-    return lax.psum(kept, axis)
+    return begin_the_plane(axis, kept)
 
 
 def passed_along(block, axis, distance):

time: 635 us -> 387 us (0.61)
  the two profiles are of different devices: /device:TPU:8 before, /device:TPU:1 now
where the time goes in v1:
time: 387 us
  waiting for transfers between devices  274 us (71%)
  matrix products  40.1 us (10%)
  other arithmetic  37.2 us (10%)
  between operations  14.9 us (4%)
  starting transfers between devices  12.1 us (3%)
  local copies, waits for them, and re-layouts  7.9 us (2%)
    all_gather x1, waiting for transfers between devices, begin_the_plane(): return jax.lax.all_gather(local_block, ax_name).sum(axis=0)  266 us
    dot_general x8, matrix products, partial_softmax(): jnp.dot(weights, value_rows, preferred_element_type=jnp.float32)  20.2 us
    dot_general x8, matrix products, partial_softmax(): lax.dot_general(query_head, key_rows, (((1,), (1,)), ((), ())), preferred...  19.9 us
    reduce_sum x8, other arithmetic, partial_softmax(): totals = jnp.sum(expons, axis=1, keepdims=True)  18.4 us
    reduce_sum x1, other arithmetic, begin_the_plane(): return jax.lax.all_gather(local_block, ax_name).sum(axis=0)  11.4 us
    all_to_all x1, waiting for transfers between devices, shards(): lax.all_to_all(fetched, 'tensor', split_axis=3, concat_axis=1, tiled=True)  8.57 us
    ppermute x2, starting transfers between devices, passed_along(): return lax.ppermute(block, axis, route)  8.13 us
  transfers between devices with their start and end apart: 4, of which 2 were waited for; matrix products, arithmetic and copies ran while one was open for 5% of the time, Pallas kernels for 0%

profile of v1, /device:TPU:1, one launch (start us, length us, event | category | flops | bytes accessed | tf_op | source)
XLA Modules:
  0.0 386.7 jit_solution(10874893331683096867)
XLA Ops:
  6.5 0.0 copy-start
  6.5 0.0 all-gather.3.cloned.1.call-start
  7.2 2.1 copy_select_fusion
  9.3 0.0 all-gather.3.cloned.1.call-update
  9.3 6.2 %collective-permute-start = (bf16[1,2,256,128]{3,2,1,0:T(8,128)(2,1)}, bf16[1,2,256,128]{3,2,1,0:T(8,128)(2,1)S(1)}, u32[]{:S(2)}, u32[]{:S(2)}) collective-permute-start(bf16[1,2,256,128]{3,2,1,0:T(8,128)(2,1)} %param.11), channel_id=1, source_target_pairs={{0,8},{8,16},{16,24},{24,32},{32,40},{40,48},{48,56},{56,64},{64,7... | collective-permute-start | bytes 393224 | tf_op jit(solution)/shard_map/ppermute | solution.py:23
  15.5 1.9 collective-permute-start.1
  17.5 2.6 copy.16
  20.7 0.2 iota_compare_fusion
  20.9 0.0 copy-done
  21.0 0.0 collective-permute-done.1
  21.0 0.6 iota_compare_fusion.2
  21.6 265.6 %all-gather.3.cloned.1.call-done = bf16[64,128,2,1024]{3,1,2,0:T(8,128)(2,1)} async-done(((bf16[1,128,2,1024]{3,1,2,0:T(8,128)(2,1)}), bf16[64,128,2,1024]{3,1,2,0:T(8,128)(2,1)}) %all-gather.3.cloned.1.call-update) | async-done | bytes 33554448 | tf_op jit(solution)/shard_map/all_gather | solution.py:12
  287.2 11.4 %reduce.2 = bf16[128,2,1024]{2,0,1:T(8,128)(2,1)S(1)} reduce(bf16[64,128,2,1024]{3,1,2,0:T(8,128)(2,1)} %all-gather.3.cloned.1.call-done, bf16[]{:T(256)} %constant.58.clone.1), dimensions={0}, to_apply=%region_0.1 | reduce | flops 16515072 | bytes 34078720 | tf_op jit(solution)/shard_map/reduce_sum | solution.py:12
  298.6 0.5 copy.31
  299.2 1.9 copy.19
  301.0 4.0 %all-to-all-start = ((bf16[1,128,2,1024]{1,2,0,3:T(2,128)(2,1)}), bf16[1,128,2,1024]{1,2,0,3:T(2,128)(2,1)S(1)}, u32[]{:S(2)}, u32[]{:S(2)}) async-start(bf16[1,128,2,1024]{1,2,0,3:T(2,128)(2,1)} %copy.19), calls=%async_computation | async-start | bytes 1048576 | tf_op jit(solution)/shard_map/all_to_all | solution.py:66
  305.0 0.6 pad_add_fusion
  305.6 0.0 collective-permute-done
  305.6 8.6 %all-to-all-done = bf16[1,128,2,1024]{1,2,0,3:T(2,128)(2,1)S(1)} async-done(((bf16[1,128,2,1024]{1,2,0,3:T(2,128)(2,1)}), bf16[1,128,2,1024]{1,2,0,3:T(2,128)(2,1)S(1)}, u32[]{:S(2)}, u32[]{:S(2)}) %all-to-all-start) | async-done | bytes 524320 | tf_op jit(solution)/shard_map/all_to_all | solution.py:66
  314.2 0.1 copy.20
  314.3 0.3 copy.21
  314.6 0.1 maximum_bitcast_fusion
  314.7 59.5 %while.13 = (s32[]{:T(128)}, f32[8,768,1]{1,0,2:T(8,128)S(1)}, f32[8,768,128]{2,1,0:T(8,128)}, bf16[8,768,128]{1,2,0:T(8,128)(2,1)}, bf16[1,2048,128]{2,1,0:T(8,...) while((s32[]{:T(128)}, f32[8,768,1]{1,0,2:T(8,128)S(1)}, ...), condition=%wide.region_4.5_spmd, body=%wide.region_1.4_spmd.sunk | while | flops 825752064 | bytes 25257056 | solution.py:57
  314.7 2.5 fusion.27
  317.2 2.5 fusion.29
  319.7 2.3 fusion.28
  322.0 0.1 dynamic_update_slice.14
  322.1 2.5 fusion.27
  324.6 2.5 fusion.29
  327.1 2.3 fusion.28
  329.4 0.1 dynamic_update_slice.14
  329.5 2.5 fusion.27
  332.0 2.5 fusion.29
  334.6 2.3 fusion.28
  336.9 0.1 dynamic_update_slice.14
  337.0 2.5 fusion.27
  339.5 2.5 fusion.29
  342.0 2.3 fusion.28
  344.3 0.1 dynamic_update_slice.14
  344.4 2.5 fusion.27
  346.9 2.5 fusion.29
  349.4 2.3 fusion.28
  351.7 0.1 dynamic_update_slice.14
  351.8 2.5 fusion.27
  354.3 2.5 fusion.29
  356.8 2.3 fusion.28
  359.2 0.1 dynamic_update_slice.14
  359.3 2.5 fusion.27
  361.7 2.6 fusion.29
  364.3 2.3 fusion.28
  366.6 0.1 dynamic_update_slice.14
  366.7 2.5 fusion.27
  369.2 2.5 fusion.29
  371.7 2.3 fusion.28
  374.0 0.1 dynamic_update_slice.14
  374.1 2.4 divide_bitcast_fusion
  376.6 1.0 copy.23
  377.6 0.7 reshape.47
  378.3 1.5 select_convert_fusion
  (16 shorter events, 0.1 us)
Async XLA Ops:
  6.5 14.4 %copy-start = (bf16[1,2,768,128]{3,2,1,0:T(8,128)(2,1)S(1)}, bf16[1,2,768,128]{3,2,1,0:T(8,128)(2,1)}, u32[]{:S(2)}) copy-start(bf16[1,2,768,128]{3,2,1,0:T(8,128)(2,1)} %param.10) | copy-start | bytes 1179652
  6.5 280.7 %all-gather.3.cloned.1.call-start = ((), (), s32[]{:S(2)}) async-start(), calls=%async_computation.1 | async-start | bytes 34078720 | tf_op jit(solution)/shard_map/all_gather | solution.py:12
  9.3 296.3 %collective-permute-start = (bf16[1,2,256,128]{3,2,1,0:T(8,128)(2,1)}, bf16[1,2,256,128]{3,2,1,0:T(8,128)(2,1)S(1)}, u32[]{:S(2)}, u32[]{:S(2)}) collective-permute-start(bf16[1,2,256,128]{3,2,1,0:T(8,128)(2,1)} %param.11), channel_id=1, source_target_pairs={{0,8},{8,16},{16,24},{24,32},{32,40},{40,48},{48,56},{56,64},{64,7... | collective-permute-start | bytes 393224 | tf_op jit(solution)/shard_map/ppermute | solution.py:23
  15.5 5.4 %collective-permute-start.1 = (s32[1]{0:T(128)}, s32[1]{0:T(128)}, u32[]{:S(2)}, u32[]{:S(2)}) collective-permute-start(s32[1]{0:T(128)} %param.14), channel_id=1, source_target_pairs={{0,8},{8,16},{16,24},{24,32},{32,40},{40,48},{48,56},{56,64},{64,7... | collective-permute-start | bytes 20 | tf_op jit(solution)/shard_map/ppermute | solution.py:23
  301.0 13.1 %all-to-all-start = ((bf16[1,128,2,1024]{1,2,0,3:T(2,128)(2,1)}), bf16[1,128,2,1024]{1,2,0,3:T(2,128)(2,1)S(1)}, u32[]{:S(2)}, u32[]{:S(2)}) async-start(bf16[1,128,2,1024]{1,2,0,3:T(2,128)(2,1)} %copy.19), calls=%async_computation | async-start | bytes 1048576 | tf_op jit(solution)/shard_map/all_to_all | solution.py:66
Sparse Core Ops, SparseCore 0:
  10.6 276.5 all-gather.2
